TPU v7x, 256 devices: a whole 4x4x8 slice. The times are simulated.
256 devices in a mesh: src: 32 (over z, y), tgt: 8 (over x, core).
Axes of the slice: x: 4, y: 4, z: 8, core: 2. Of those that a mesh axis runs over, the one named last changes fastest.
Arguments:
- source: bfloat16 [32768, 300], P('src'), may hold values from -70 to 70
- target: bfloat16 [16384, 300], P('tgt'), may hold values from -11 to 11
- start_map: float32 [300, 300], replicated, may hold values from -1.5 to 1.5
Outputs:
- source_soft: bfloat16 [32768, 300], P(('src', 'tgt'))
- target_soft: bfloat16 [16384, 300], P('tgt')
- polar_map: float32 [300, 300], replicated
All inputs are finite; a program needn't handle non-finite values.
Results may differ from a plain program's by a relative error of at most 0.014.
The roundings to bfloat16 on the way count: a program that leaves them out, or rounds other values in their place, can miss the bound.
Values may be sent and summed in bfloat16 or wider, within the bound.
A program may use at most 64 MiB of HBM per device.

v0:
```python
import math
import jax
import jax.numpy as jnp
from jax import lax
from jax.sharding import PartitionSpec as P

ITERS = 2
NEWTON_STEPS = 8


def polar_steps(covariance):
    highest = lax.Precision.HIGHEST
    current = covariance / jnp.sqrt(jnp.sum(covariance * covariance) + 1e-06)
    for newton in range(NEWTON_STEPS):
        gram_matrix = jnp.dot(current.T, current, precision=highest)
        current = 1.5 * current - 0.5 * jnp.dot(current, gram_matrix, precision=highest)
    return current


def translation_sums(row_weights, col_weights, source, target, share_target, src_index):
    source_sum = lax.psum_scatter(
        jnp.dot(row_weights, target, preferred_element_type=jnp.float32),
        "tgt",
        scatter_dimension=0,
        tiled=True,
    )
    target_full = lax.psum(
        lax.dot_general(
            col_weights, source, (((0,), (0,)), ((), ())), preferred_element_type=jnp.float32
        ),
        "src",
    )
    target_sum = lax.dynamic_slice_in_dim(target_full, src_index * share_target, share_target, 0)
    return (source_sum, target_sum, target_full)


def body(source, target, start_map):
    highest = lax.Precision.HIGHEST
    score_scale = 2.0 / math.sqrt(source.shape[1])
    rows_source = source.shape[0]
    rows_target = target.shape[0]
    src_devices = lax.axis_size("src")
    tgt_devices = lax.axis_size("tgt")
    src_index = lax.axis_index("src")
    tgt_index = lax.axis_index("tgt")
    share_source = rows_source // tgt_devices
    share_target = rows_target // src_devices
    source_piece = lax.dynamic_slice_in_dim(
        source, tgt_index * share_source, share_source, 0
    ).astype(jnp.float32)
    target_piece = lax.dynamic_slice_in_dim(
        target, src_index * share_target, share_target, 0
    ).astype(jnp.float32)
    current = start_map
    source_sum = None
    target_sum = None
    target_full = None
    for iteration in range(ITERS):
        mapped = jnp.dot(
            source, current.astype(jnp.bfloat16), preferred_element_type=jnp.float32
        ).astype(jnp.bfloat16)
        scores = (
            lax.dot_general(
                mapped, target, (((1,), (1,)), ((), ())), preferred_element_type=jnp.float32
            )
            * score_scale
        )
        row_local = jnp.max(scores, axis=1)
        col_local = jnp.max(scores, axis=0)
        row_top = lax.pmax(row_local, "tgt")
        col_top = lax.pmax(col_local, "src")
        row_total = lax.psum(jnp.sum(jnp.exp(scores - row_top[:, None]), axis=1), "tgt")
        col_total = lax.psum(jnp.sum(jnp.exp(scores - col_top[None, :]), axis=0), "src")
        row_weights = (jnp.exp(scores - row_top[:, None]) / row_total[:, None]).astype(jnp.bfloat16)
        col_weights = (jnp.exp(scores - col_top[None, :]) / col_total[None, :]).astype(jnp.bfloat16)
        source_sum, target_sum, target_full = translation_sums(
            row_weights, col_weights, source, target, share_target, src_index
        )
        covariance = jnp.dot(source_piece.T, source_sum, precision=highest)
        covariance = covariance + jnp.dot(target_sum.T, target_piece, precision=highest)
        covariance = lax.psum(covariance, ("src", "tgt"))
        current = polar_steps(covariance)
    source_share = source_sum.astype(jnp.bfloat16)
    target_soft = target_full.astype(jnp.bfloat16)
    return (source_share, target_soft, current)


def solution(mesh):
    in_specs = (P("src", None), P("tgt", None), P())
    out_specs = (P(("src", "tgt"), None), P("tgt", None), P())
    return jax.shard_map(body, mesh=mesh, in_specs=in_specs, out_specs=out_specs, check_vma=False)
```

profile of v0, /device:TPU:2, one launch (start us, length us, event | category | flops | bytes accessed | tf_op | source)
XLA Modules:
  0.0 1263.8 jit_solution(214851185553863919)
XLA Ops:
  9.3 7.3 multiply_reduce_fusion.2
  16.6 78.9 %pmax.29 = f32[2048]{0:T(1024)S(1)} all-reduce(f32[2048]{0:T(1024)S(1)} %get-tuple-element.9), channel_id=1, replica_groups=mesh['src'=32,'tgt'=8] {'src'}, use_global_device_ids=true, to_apply=%region_6.0 | all-reduce | flops 2048 | bytes 16384 | tf_op jit(solution)/shard_map/pmax | solution.py:71
  95.5 10.0 pmax.28
  105.6 5.2 fusion.1
  110.8 12.4 psum.56
  123.2 7.0 fusion.6
  130.3 70.6 %psum.57 = f32[2048]{0:T(1024)S(1)} all-reduce(f32[2048]{0:T(1024)S(1)} %get-tuple-element.7), channel_id=1, replica_groups=mesh['src'=32,'tgt'=8] {'src'}, use_global_device_ids=true, to_apply=%region_8.0 | all-reduce | flops 2048 | bytes 16384 | tf_op jit(solution)/shard_map/psum | solution.py:73
  201.0 7.6 fusion.4
  210.0 153.4 %all-reduce.5.cloned.1.call-done = f32[2048,300]{1,0:T(8,128)} async-done(((f32[2048,300]{1,0:T(8,128)}), f32[2048,300]{1,0:T(8,128)}) %all-reduce.5.cloned.1.call-update) | async-done | bytes 2457616 | tf_op jit(solution)/shard_map/psum | solution.py:27
  365.8 248.9 %all-reduce.7.cloned.1.call-done = f32[300,300]{1,0:T(8,128)} async-done(((f32[300,300]{1,0:T(8,128)}), f32[300,300]{1,0:T(8,128)}) %all-reduce.7.cloned.1.call-update) | async-done | bytes 360016 | tf_op jit(solution)/shard_map/psum | solution.py:81
  617.1 2.4 fusion.29
  638.2 5.3 multiply_reduce_fusion
  643.5 72.1 %pmax.31 = f32[2048]{0:T(1024)S(1)} all-reduce(f32[2048]{0:T(1024)S(1)} %get-tuple-element.5), channel_id=1, replica_groups=mesh['src'=32,'tgt'=8] {'src'}, use_global_device_ids=true, to_apply=%region_18.0 | all-reduce | flops 2048 | bytes 16384 | tf_op jit(solution)/shard_map/pmax | solution.py:71
  715.6 10.0 pmax.30
  725.6 5.2 fusion.3
  730.9 12.6 %psum.60 = f32[1024]{0:T(1024)S(1)} all-reduce(f32[1024]{0:T(1024)S(1)} %get-tuple-element.4), channel_id=1, replica_groups=mesh['src'=32,'tgt'=8] {'tgt'}, use_global_device_ids=true, to_apply=%region_15.0 | all-reduce | flops 1024 | bytes 8192 | tf_op jit(solution)/shard_map/psum | solution.py:72
  743.5 6.4 fusion.7
  750.0 70.8 %psum.61 = f32[2048]{0:T(1024)S(1)} all-reduce(f32[2048]{0:T(1024)S(1)} %get-tuple-element.3), channel_id=1, replica_groups=mesh['src'=32,'tgt'=8] {'src'}, use_global_device_ids=true, to_apply=%region_20.0 | all-reduce | flops 2048 | bytes 16384 | tf_op jit(solution)/shard_map/psum | solution.py:73
  820.8 6.8 fusion.5
  829.2 151.9 %all-reduce.9.cloned.1.call-done = f32[2048,300]{0,1:T(8,128)} async-done(((f32[2048,300]{0,1:T(8,128)}), f32[2048,300]{0,1:T(8,128)}) %all-reduce.9.cloned.1.call-update) | async-done | bytes 2457616 | tf_op jit(solution)/shard_map/psum | solution.py:27
  984.8 2.9 convert_element_type.42
  987.7 244.7 %all-reduce.11.cloned.1.call-done = f32[300,300]{1,0:T(8,128)} async-done(((f32[300,300]{1,0:T(8,128)}), f32[300,300]{1,0:T(8,128)}) %all-reduce.11.cloned.1.call-update) | async-done | bytes 360016 | tf_op jit(solution)/shard_map/psum | solution.py:81
  1234.8 2.4 fusion.30
  1237.2 2.2 fusion.17
  (54 shorter events, 49.3 us)
Async XLA Ops:
  8.0 1.3 copy-start
  8.0 200.7 %reduce-scatter.3.cloned.1.call-start = ((), (), s32[]{:S(2)}) async-start(), calls=%async_computation.2 | async-start | bytes 1769472 | tf_op jit(solution)/shard_map/reduce_scatter | solution.py:21
  123.2 77.8 %copy-start.1 = (bf16[1024,300]{0,1:T(8,128)(2,1)S(1)}, bf16[1024,300]{0,1:T(8,128)(2,1)}, u32[]{:S(2)}) copy-start(bf16[1024,300]{0,1:T(8,128)(2,1)} %param.3) | copy-start | bytes 1843204
  130.3 233.1 %all-reduce.5.cloned.1.call-start = ((), (), s32[]{:S(2)}) async-start(), calls=%async_computation.3 | async-start | bytes 6291456 | tf_op jit(solution)/shard_map/psum | solution.py:27
  208.6 406.1 %all-reduce.7.cloned.1.call-start = ((), (), s32[]{:S(2)}) async-start(), calls=%async_computation.4 | async-start | bytes 933888 | tf_op jit(solution)/shard_map/psum | solution.py:81
  365.5 462.4 %reduce-scatter.5.cloned.1.call-start = ((), (), s32[]{:S(2)}) async-start(), calls=%async_computation.5 | async-start | bytes 1400832 | tf_op jit(solution)/shard_map/reduce_scatter | solution.py:21
  749.9 231.1 %all-reduce.9.cloned.1.call-start = ((), (), s32[]{:S(2)}) async-start(), calls=%async_computation.6 | async-start | bytes 4980736 | tf_op jit(solution)/shard_map/psum | solution.py:27
  827.7 404.7 %all-reduce.11.cloned.1.call-start = ((), (), s32[]{:S(2)}) async-start(), calls=%async_computation.7 | async-start | bytes 933888 | tf_op jit(solution)/shard_map/psum | solution.py:81
Sparse Core Ops, SparseCore 0:
  130.4 26.5 reduce-scatter.2
  365.6 248.9 all-reduce.6
  750.1 27.8 reduce-scatter.4
  983.3 249.0 all-reduce.10
Sparse Core Ops, SparseCore 1:
  208.7 154.6 all-reduce.4
  827.8 153.2 all-reduce.8
where the time goes:
time: 1270 us; the launch traced here: 1260 us
  waiting for transfers between devices  799 us (63%)
  blocking collectives  338 us (27%)
  matrix products  89.8 us (7%)
  other arithmetic  18.4 us (1%)
  between operations  17.2 us (1%)
    psum x2, waiting for transfers between devices, body(): covariance = lax.psum(covariance, ('src', 'tgt'))  494 us
    psum x2, waiting for transfers between devices, translation_sums(): lax.psum(lax.dot_general(col_weights, source, (((0,), (0,)), ((), ())), p...  305 us
    pmax x2, blocking collectives, body(): col_top = lax.pmax(col_local, 'src')  151 us
    psum x2, blocking collectives, body(): lax.psum(jnp.sum(jnp.exp(scores - col_top[None, :]), axis=0), 'src')  141 us
  transfers between devices with their start and end apart: 6, of which 4 were waited for; matrix products, arithmetic and copies ran while one was open for 2% of the time, Pallas kernels for 0%

commit v1 on v0

--- a/solution.py
+++ b/solution.py
@@ -78,7 +78,7 @@
         )
         covariance = jnp.dot(source_piece.T, source_sum, precision=highest)
         covariance = covariance + jnp.dot(target_sum.T, target_piece, precision=highest)
-        covariance = lax.psum(covariance, ("src", "tgt"))
+        covariance = lax.psum(lax.psum(covariance, "src"), "tgt")
         current = polar_steps(covariance)
     source_share = source_sum.astype(jnp.bfloat16)
     target_soft = target_full.astype(jnp.bfloat16)

time: 1270 us -> 1210 us (0.953)
  waiting for transfers between devices: 799 us -> 714 us
    psum x2 -> x4, waiting for transfers between devices: 494 us -> 408 us  [body(): covariance = lax.psum(lax.psum(covariance, 'src'), 'tgt')]
  transfers between devices with their start and end apart: 6 -> 8, of which waited for: 4 -> 6; matrix products, arithmetic and copies ran while one was open for 2% -> 2% of each run, Pallas kernels for 0% -> 0%
where the time goes in v1:
time: 1210 us; the launch traced here: 1200 us
  waiting for transfers between devices  714 us (59%)
  blocking collectives  344 us (28%)
  matrix products  99.5 us (8%)
  other arithmetic  18.4 us (2%)
  between operations  17.7 us (1%)
    psum x4, waiting for transfers between devices, body(): covariance = lax.psum(lax.psum(covariance, 'src'), 'tgt')  408 us
    psum x2, waiting for transfers between devices, translation_sums(): lax.psum(lax.dot_general(col_weights, source, (((0,), (0,)), ((), ())), p...  305 us
    pmax x2, blocking collectives, body(): col_top = lax.pmax(col_local, 'src')  155 us
    psum x2, blocking collectives, body(): lax.psum(jnp.sum(jnp.exp(scores - col_top[None, :]), axis=0), 'src')  141 us
    dot_general x16, matrix products, polar_steps(): gram_matrix = jnp.dot(current.T, current, precision=highest)  32.4 us
    psum x2, blocking collectives, body(): lax.psum(jnp.sum(jnp.exp(scores - row_top[:, None]), axis=1), 'tgt')  25.3 us
  transfers between devices with their start and end apart: 8, of which 6 were waited for; matrix products, arithmetic and copies ran while one was open for 2% of the time, Pallas kernels for 0%

profile of v1, /device:TPU:2, one launch (start us, length us, event | category | flops | bytes accessed | tf_op | source)
XLA Modules:
  0.0 1195.5 jit_solution(12933933521449382833)
XLA Ops:
  9.3 7.3 multiply_reduce_fusion.2
  16.6 78.9 %pmax.29 = f32[2048]{0:T(1024)S(1)} all-reduce(f32[2048]{0:T(1024)S(1)} %get-tuple-element.9), channel_id=1, replica_groups=mesh['src'=32,'tgt'=8] {'src'}, use_global_device_ids=true, to_apply=%region_6.0 | all-reduce | flops 2048 | bytes 16384 | tf_op jit(solution)/shard_map/pmax | solution.py:71
  95.5 10.0 pmax.28
  105.6 5.2 fusion.1
  110.8 12.4 %psum.70 = f32[1024]{0:T(1024)S(1)} all-reduce(f32[1024]{0:T(1024)S(1)} %get-tuple-element.8), channel_id=1, replica_groups=mesh['src'=32,'tgt'=8] {'tgt'}, use_global_device_ids=true, to_apply=%region_3.0 | all-reduce | flops 1024 | bytes 8192 | tf_op jit(solution)/shard_map/psum | solution.py:72
  123.2 7.0 fusion.6
  130.3 70.6 %psum.71 = f32[2048]{0:T(1024)S(1)} all-reduce(f32[2048]{0:T(1024)S(1)} %get-tuple-element.7), channel_id=1, replica_groups=mesh['src'=32,'tgt'=8] {'src'}, use_global_device_ids=true, to_apply=%region_8.0 | all-reduce | flops 2048 | bytes 16384 | tf_op jit(solution)/shard_map/psum | solution.py:73
  201.0 7.6 fusion.4
  210.0 153.3 %all-reduce.7.cloned.1.call-done = f32[2048,300]{1,0:T(8,128)} async-done(((f32[2048,300]{1,0:T(8,128)}), f32[2048,300]{1,0:T(8,128)}) %all-reduce.7.cloned.1.call-update) | async-done | bytes 2457616 | tf_op jit(solution)/shard_map/psum | solution.py:27
  365.5 146.2 %all-reduce.9.cloned.1.call-done = f32[300,300]{1,0:T(8,128)} async-done(((f32[300,300]{1,0:T(8,128)}), f32[300,300]{1,0:T(8,128)}) %all-reduce.9.cloned.1.call-update) | async-done | bytes 360016 | tf_op jit(solution)/shard_map/psum | solution.py:81
  512.0 60.0 %all-reduce.11.cloned.1.call-done = f32[300,300]{1,0:T(8,128)} async-done(((f32[300,300]{1,0:T(8,128)}), f32[300,300]{1,0:T(8,128)}) %all-reduce.11.cloned.1.call-update) | async-done | bytes 360016 | tf_op jit(solution)/shard_map/psum | solution.py:81
  588.3 11.2 fusion.53
  605.2 5.3 multiply_reduce_fusion
  610.5 76.1 %pmax.31 = f32[2048]{0:T(1024)S(1)} all-reduce(f32[2048]{0:T(1024)S(1)} %get-tuple-element.5), channel_id=1, replica_groups=mesh['src'=32,'tgt'=8] {'src'}, use_global_device_ids=true, to_apply=%region_19.0 | all-reduce | flops 2048 | bytes 16384 | tf_op jit(solution)/shard_map/pmax | solution.py:71
  686.6 12.3 %pmax.30 = f32[1024]{0:T(1024)S(1)} all-reduce(f32[1024]{0:T(1024)S(1)} %get-tuple-element.6), channel_id=1, replica_groups=mesh['src'=32,'tgt'=8] {'tgt'}, use_global_device_ids=true, to_apply=%region_14.0 | all-reduce | flops 1024 | bytes 8192 | tf_op jit(solution)/shard_map/pmax | solution.py:70
  698.9 5.2 fusion.3
  704.2 12.9 %psum.75 = f32[1024]{0:T(1024)S(1)} all-reduce(f32[1024]{0:T(1024)S(1)} %get-tuple-element.4), channel_id=1, replica_groups=mesh['src'=32,'tgt'=8] {'tgt'}, use_global_device_ids=true, to_apply=%region_16.0 | all-reduce | flops 1024 | bytes 8192 | tf_op jit(solution)/shard_map/psum | solution.py:72
  717.1 6.4 fusion.7
  723.6 70.6 %psum.76 = f32[2048]{0:T(1024)S(1)} all-reduce(f32[2048]{0:T(1024)S(1)} %get-tuple-element.3), channel_id=1, replica_groups=mesh['src'=32,'tgt'=8] {'src'}, use_global_device_ids=true, to_apply=%region_21.0 | all-reduce | flops 2048 | bytes 16384 | tf_op jit(solution)/shard_map/psum | solution.py:73
  794.3 6.8 fusion.5
  802.5 152.1 %all-reduce.13.cloned.1.call-done = f32[2048,300]{0,1:T(8,128)} async-done(((f32[2048,300]{0,1:T(8,128)}), f32[2048,300]{0,1:T(8,128)}) %all-reduce.13.cloned.1.call-update) | async-done | bytes 2457616 | tf_op jit(solution)/shard_map/psum | solution.py:27
  957.0 146.3 %all-reduce.15.cloned.1.call-done = f32[300,300]{1,0:T(8,128)} async-done(((f32[300,300]{1,0:T(8,128)}), f32[300,300]{1,0:T(8,128)}) %all-reduce.15.cloned.1.call-update) | async-done | bytes 360016 | tf_op jit(solution)/shard_map/psum | solution.py:81
  1104.9 2.9 convert_element_type.42
  1107.8 55.8 %all-reduce.17.cloned.1.call-done = f32[300,300]{1,0:T(8,128)} async-done(((f32[300,300]{1,0:T(8,128)}), f32[300,300]{1,0:T(8,128)}) %all-reduce.17.cloned.1.call-update) | async-done | bytes 360016 | tf_op jit(solution)/shard_map/psum | solution.py:81
  (60 shorter events, 55.0 us)
Async XLA Ops:
  8.0 1.3 copy-start
  8.0 200.7 %reduce-scatter.3.cloned.1.call-start = ((), (), s32[]{:S(2)}) async-start(), calls=%async_computation.2 | async-start | bytes 1769472 | tf_op jit(solution)/shard_map/reduce_scatter | solution.py:21
  123.2 77.8 %copy-start.1 = (bf16[1024,300]{0,1:T(8,128)(2,1)S(1)}, bf16[1024,300]{0,1:T(8,128)(2,1)}, u32[]{:S(2)}) copy-start(bf16[1024,300]{0,1:T(8,128)(2,1)} %param.3) | copy-start | bytes 1843204
  130.3 233.0 %all-reduce.7.cloned.1.call-start = ((), (), s32[]{:S(2)}) async-start(), calls=%async_computation.3 | async-start | bytes 6291456 | tf_op jit(solution)/shard_map/psum | solution.py:27
  208.6 303.1 %all-reduce.9.cloned.1.call-start = ((), (), s32[]{:S(2)}) async-start(), calls=%async_computation.4 | async-start | bytes 933888 | tf_op jit(solution)/shard_map/psum | solution.py:81
  365.5 206.6 %all-reduce.11.cloned.1.call-start = ((), (), s32[]{:S(2)}) async-start(), calls=%async_computation.5 | async-start | bytes 933888 | tf_op jit(solution)/shard_map/psum | solution.py:81
  511.7 289.5 %reduce-scatter.5.cloned.1.call-start = ((), (), s32[]{:S(2)}) async-start(), calls=%async_computation.6 | async-start | bytes 1400832 | tf_op jit(solution)/shard_map/reduce_scatter | solution.py:21
  723.6 231.0 %all-reduce.13.cloned.1.call-start = ((), (), s32[]{:S(2)}) async-start(), calls=%async_computation.7 | async-start | bytes 4980736 | tf_op jit(solution)/shard_map/psum | solution.py:27
  801.1 302.1 %all-reduce.15.cloned.1.call-start = ((), (), s32[]{:S(2)}) async-start(), calls=%async_computation.8 | async-start | bytes 933888 | tf_op jit(solution)/shard_map/psum | solution.py:81
  956.7 206.9 %all-reduce.17.cloned.1.call-start = ((), (), s32[]{:S(2)}) async-start(), calls=%async_computation.9 | async-start | bytes 933888 | tf_op jit(solution)/shard_map/psum | solution.py:81
Sparse Core Ops, SparseCore 0:
  130.4 26.5 reduce-scatter.2
  511.8 60.1 all-reduce.10
  723.7 27.6 reduce-scatter.4
  1103.4 60.1 all-reduce.16
Sparse Core Ops, SparseCore 1:
  208.7 154.5 all-reduce.6
  367.5 144.2 all-reduce.8
  801.2 153.3 all-reduce.12
  958.9 144.3 all-reduce.14
